TPU v7x, 256 devices: a whole 4x4x8 slice. The times are simulated.
256 devices in a mesh: frame: 16 (over x, z_lo), fsdp: 16 (over z_hi, y, core).
Axes of the slice: x: 4, y: 4, z: 8 (z_hi: 2, z_lo: 4; z = z_hi * 4 + z_lo), core: 2. Of those that a mesh axis runs over, the one named last changes fastest.
Arguments:
- queries: bfloat16 [256, 192, 3072], P(('frame', 'fsdp')), may hold values from -18 to 18
- keys: bfloat16 [256, 192, 3072], P(('frame', 'fsdp')), may hold values from -7 to 7
- values: bfloat16 [256, 192, 3072], P(('frame', 'fsdp')), may hold values from -6 to 6
- residual: bfloat16 [256, 192, 3072], P(('frame', 'fsdp')), may hold values from -6 to 6
- target: bfloat16 [256, 192, 3072], P(('frame', 'fsdp')), may hold values from -6 to 6
- output_weight: bfloat16 [3072, 3072], P('fsdp'), may hold values from -0.109375 to 0.109375
- down_adapter: bfloat16 [16, 64, 3072], P('frame', None, 'fsdp'), may hold values from -0.109375 to 0.109375
- up_adapter: bfloat16 [16, 64, 3072], P('frame', None, 'fsdp'), may hold values from -1.1953125 to 1.1953125
- scene_of_frame: int32 [256], P(('frame', 'fsdp')), may hold values from 0 to 15
- scene_adapter_row: int32 [16], replicated, may hold values from 0 to 15, each once
- valid_token_count: int32 [256], P(('frame', 'fsdp')), may hold values from 1 to 192, 30720 in all
Outputs:
- grad_down: float32 [16, 64, 3072], P('frame', None, 'fsdp')
- grad_up: float32 [16, 64, 3072], P('frame', None, 'fsdp')
- frame_loss: float32 [256], P(('frame', 'fsdp'))
Inputs may be any that keep to these rules, and one draw needn't show every extreme that they name: `scene_adapter_row`: each scene has its own adapter row. `valid_token_count`: some frame has all 192 slots valid.
All inputs are finite; a program needn't handle non-finite values. No bound on the sum of `valid_token_count` on one device may be relied on, other than what follows from the above.
Results may differ from a plain program's by a relative error of at most 0.0053.
Values may be sent and summed in bfloat16 or wider, within the bound.
A program may use at most 192 MiB of HBM per device.

v0:
```python
import math
import jax
import jax.numpy as jnp
from jax import lax
from jax.sharding import PartitionSpec as P

HEADS = 24
adapter_scale = 2.0


def slot_lookup(scene_ids, scene_adapter_row):
    scene_range = jnp.arange(scene_adapter_row.shape[0], dtype=jnp.int32)
    matches = scene_ids[:, None] == scene_range[None, :]
    return jnp.sum(jnp.where(matches, scene_adapter_row[None, :], 0), axis=1)


def per_device(
    queries,
    keys,
    values,
    residual,
    target,
    output_weight,
    down_adapter,
    up_adapter,
    scene_of_frame,
    scene_adapter_row,
    valid_token_count,
):
    frames, slot_count, model_width = queries.shape
    head_count = HEADS
    head_size = model_width // head_count
    row_count = frames * slot_count
    score_scale = 1.0 / math.sqrt(head_size)
    query_heads = queries.reshape(frames, slot_count, head_count, head_size)
    key_heads = keys.reshape(frames, slot_count, head_count, head_size)
    value_heads = values.reshape(frames, slot_count, head_count, head_size)
    scores = (
        jnp.einsum("fqhd,fkhd->fhqk", query_heads, key_heads, preferred_element_type=jnp.float32)
        * score_scale
    )
    positions = lax.broadcasted_iota(jnp.int32, (frames, slot_count), 1)
    valid_mask = positions < valid_token_count[:, None]
    scores = jnp.where(valid_mask[:, None, None, :], scores, -jnp.inf)
    row_max = jnp.max(scores, axis=-1, keepdims=True)
    exponent = jnp.exp(scores - row_max)
    weights = (exponent / jnp.sum(exponent, axis=-1, keepdims=True)).astype(jnp.bfloat16)
    attended = jnp.einsum(
        "fhqk,fkhd->fqhd", weights, value_heads, preferred_element_type=jnp.float32
    )
    attended = attended.astype(jnp.bfloat16).reshape(frames, slot_count, model_width)
    mixed_flat = attended.reshape(row_count, model_width)
    projected_tokens = jnp.dot(
        mixed_flat,
        lax.all_gather(output_weight, "fsdp", axis=0, tiled=True),
        preferred_element_type=jnp.float32,
    )
    projected_tokens = projected_tokens.reshape(frames, slot_count, model_width)
    column_ids = lax.all_gather(scene_of_frame, "fsdp", axis=0, tiled=True)
    column_slots = slot_lookup(column_ids, scene_adapter_row)
    owner_range = jnp.arange(scene_adapter_row.shape[0], dtype=jnp.int32)
    column_pick = column_slots[:, None] == owner_range[None, :]
    adapter_couple = jnp.stack([down_adapter, up_adapter], axis=1)
    blocks = lax.all_gather(adapter_couple, "frame", axis=0, tiled=True)
    chosen = jnp.einsum(
        "fs,sxrd->fxrd",
        column_pick.astype(jnp.bfloat16),
        blocks,
        preferred_element_type=jnp.float32,
    )
    adapters = lax.all_to_all(
        chosen.astype(jnp.bfloat16), "fsdp", split_axis=0, concat_axis=3, tiled=True
    )
    down_weight_rows = adapters[:, 0]
    up_weight_rows = adapters[:, 1]
    low_rank_state = jnp.einsum(
        "ftd,frd->ftr", attended, down_weight_rows, preferred_element_type=jnp.float32
    ).astype(jnp.bfloat16)
    adapter_output = jnp.einsum(
        "akw,awe->ake", low_rank_state, up_weight_rows, preferred_element_type=jnp.float32
    )
    combined_output = (
        residual.astype(jnp.float32)
        + projected_tokens
        + adapter_scale * adapter_output
        - target.astype(jnp.float32)
    )
    residual_error = jnp.where(
        valid_mask[:, :, None], combined_output, jnp.zeros_like(combined_output)
    )
    token_float = valid_token_count.astype(jnp.float32)
    frame_loss = jnp.sum(residual_error * residual_error, axis=(1, 2)) / (token_float * model_width)
    output_gradient = (2.0 * residual_error / token_float[:, None, None]).astype(jnp.bfloat16)
    up_gradient_terms = adapter_scale * jnp.einsum(
        "ftr,ftd->frd", low_rank_state, output_gradient, preferred_element_type=jnp.float32
    )
    backward_low_rank = (
        adapter_scale
        * jnp.einsum(
            "ftd,frd->ftr", output_gradient, up_weight_rows, preferred_element_type=jnp.float32
        )
    ).astype(jnp.bfloat16)
    down_terms = jnp.einsum(
        "ftr,ftd->frd", backward_low_rank, attended, preferred_element_type=jnp.float32
    )
    grad_terms = jnp.stack([down_terms, up_gradient_terms], axis=1)
    pieces = lax.all_to_all(grad_terms, "fsdp", split_axis=3, concat_axis=0, tiled=True)
    scene_dense = jnp.einsum(
        "fs,fxrd->sxrd", column_pick.astype(jnp.float32), pieces, precision=lax.Precision.HIGHEST
    )
    scene_full = lax.psum(scene_dense, "frame")
    owned_rows = lax.dynamic_slice_in_dim(scene_full, lax.axis_index("frame"), 1, 0)
    return (owned_rows[:, 0], owned_rows[:, 1], frame_loss)


def solution(mesh):
    placed = (
        P(("frame", "fsdp"), None, None),
        P(("frame", "fsdp"), None, None),
        P(("frame", "fsdp"), None, None),
        P(("frame", "fsdp"), None, None),
        P(("frame", "fsdp"), None, None),
        P("fsdp", None),
        P("frame", None, "fsdp"),
        P("frame", None, "fsdp"),
        P(("frame", "fsdp")),
        P(),
        P(("frame", "fsdp")),
    )
    return jax.shard_map(
        per_device,
        mesh=mesh,
        in_specs=placed,
        out_specs=(P("frame", None, "fsdp"), P("frame", None, "fsdp"), P(("frame", "fsdp"))),
        check_vma=False,
    )
```

profile of v0, /device:TPU:16, one launch (start us, length us, event | category | flops | bytes accessed | tf_op | source)
XLA Modules:
  0.0 509.0 jit_solution(2743683499181057483)
XLA Ops:
  8.6 1.3 dynamic-slice
  9.8 0.8 dynamic-update-slice
  10.6 15.7 %all-reduce = s32[16]{0:T(128)S(1)} all-reduce(s32[16]{0:T(128)S(1)} %dynamic-update-slice), channel_id=1, replica_groups=mesh['frame'=16,'fsdp'=16] {'fsdp'}, use_global_device_ids=true, to_apply=%add | all-reduce | flops 16 | bytes 128
  26.3 0.8 select_reduce_fusion
  27.1 0.8 pad_maximum_fusion.1
  27.9 76.0 %all_gather.11 = bf16[16,2,64,192]{3,2,1,0:T(8,128)(2,1)S(1)} all-gather(bf16[1,2,64,192]{3,2,1,0:T(8,128)(2,1)S(1)} %pad_maximum_fusion.1), channel_id=1, replica_groups=mesh['frame'=16,'fsdp'=16] {'frame'}, dimensions={0}, use_global_device_ids=true | all-gather | bytes 835584 | tf_op jit(solution)/shard_map/all_gather | solution.py:64
  103.9 0.7 convolution_convert_fusion
  104.6 1.3 copy.63
  106.0 4.8 all-to-all-start
  111.7 1.6 copy.75
  113.6 0.8 fusion.24
  114.4 2.0 fusion.51
  116.3 1.1 fusion.15
  117.5 1.8 copy.60
  119.3 54.0 %all-to-all-done = bf16[16,2,64,192]{3,2,1,0:T(8,128)(2,1)S(1)} async-done(((bf16[16,2,64,192]{3,2,1,0:T(8,128)(2,1)}), bf16[16,2,64,192]{3,2,1,0:T(8,128)(2,1)S(1)}, u32[]{:S(2)}, u32[]{:S(2)}) %all-to-all-start) | async-done | bytes 786464 | tf_op jit(solution)/shard_map/all_to_all | solution.py:71
  173.9 1.1 all_to_all.29
  175.0 1.8 fusion.33
  176.8 58.8 %all-gather.2.cloned.1.call-done = bf16[3072,3072]{1,0:T(8,128)(2,1)} async-done(((bf16[192,3072]{1,0:T(8,128)(2,1)}), bf16[3072,3072]{1,0:T(8,128)(2,1)}) %all-gather.2.cloned.1.call-update) | async-done | bytes 18874384 | tf_op jit(solution)/shard_map/all_gather | solution.py:55
  235.6 9.1 %fusion.5 = f32[1,192,3072]{2,1,0:T(8,128)S(1)} fusion(bf16[3072,3072]{1,0:T(8,128)(2,1)} %all-gather.2.cloned.1.call-done, bf16[1,192,3072]{2,1,0:T(8,128)(2,1)} %param.14, bf16[24,8,24,128]{3,2,1,0:T(8,128)(2,1)S(1)} %bitcast.107), kind=kOutput, calls=%fused_computation.10 | convolution fusion | flops 3625058304 | bytes 23592960 | tf_op jit(solution)/shard_map/dot_general | solution.py:53
  244.7 1.5 multiply_reduce_fusion
  246.2 1.3 fusion.7
  247.4 3.2 convolution_bitcast_fusion.1
  250.6 2.7 pad_maximum_fusion
  253.3 4.4 copy.65
  257.8 4.2 reshape.120
  262.0 42.7 %all_to_all.36 = f32[16,1,24576]{2,1,0:T(1,128)S(1)} all-to-all(f32[16,1,24576]{2,1,0:T(1,128)} %reshape.120), channel_id=1, replica_groups=mesh['frame'=16,'fsdp'=16] {'fsdp'}, dimensions={0} | all-to-all | bytes 3145728 | tf_op jit(solution)/shard_map/all_to_all | solution.py:107
  305.2 6.0 %reduce.5 = f32[16,24576]{1,0:T(8,128)} reduce(f32[16,1,24576]{2,1,0:T(1,128)S(1)} %all_to_all.36, f32[]{:T(128)} %broadcast.46), dimensions={1}, to_apply=%all_to_all.30.reduce_sub_computation | reduce | bytes 3145732 | tf_op jit(solution)/shard_map/all_to_all | solution.py:107
  311.2 3.4 reshape.121
  314.7 3.8 copy.73
  318.5 4.0 fusion.12
  323.2 175.3 %all-reduce.3.cloned.1.call-done = f32[16,2,64,192]{3,0,2,1:T(8,128)} async-done(((f32[16,2,64,192]{3,0,2,1:T(8,128)}), f32[16,2,64,192]{3,0,2,1:T(8,128)}) %all-reduce.3.cloned.1.call-update) | async-done | bytes 1572880 | tf_op jit(solution)/shard_map/psum | solution.py:111
  498.5 1.3 dynamic-slice_bitcast_fusion
  (20 shorter events, 3.6 us)
Async XLA Ops:
  7.2 228.4 %all-gather.2.cloned.1.call-start = ((), (), s32[]{:S(2)}) async-start(), calls=%async_computation.2 | async-start | bytes 20054016 | tf_op jit(solution)/shard_map/all_gather | solution.py:55
  104.6 6.9 %copy-start = (bf16[1,192,3072]{2,1,0:T(8,128)(2,1)S(1)}, bf16[1,192,3072]{2,1,0:T(8,128)(2,1)}, u32[]{:S(2)}) copy-start(bf16[1,192,3072]{2,1,0:T(8,128)(2,1)} %param.11) | copy-start | bytes 3538948
  106.0 67.3 %all-to-all-start = ((bf16[16,2,64,192]{3,2,1,0:T(8,128)(2,1)}), bf16[16,2,64,192]{3,2,1,0:T(8,128)(2,1)S(1)}, u32[]{:S(2)}, u32[]{:S(2)}) async-start(bf16[16,2,64,192]{3,2,1,0:T(8,128)(2,1)} %copy.63), calls=%async_computation | async-start | bytes 2097152 | tf_op jit(solution)/shard_map/all_to_all | solution.py:71
  110.8 387.7 %all-reduce.3.cloned.1.call-start = ((), (), s32[]{:S(2)}) async-start(), calls=%async_computation.3 | async-start | bytes 4194304 | tf_op jit(solution)/shard_map/psum | solution.py:111
  111.5 1.8 copy-start.1
  173.9 61.7 %copy-start.2 = (bf16[1,192,24,128]{3,2,1,0:T(8,128)(2,1)S(1)}, bf16[1,192,24,128]{3,2,1,0:T(8,128)(2,1)}, u32[]{:S(2)}) copy-start(bf16[1,192,24,128]{3,2,1,0:T(8,128)(2,1)} %copy.60) | copy-start | bytes 3538948
  235.6 9.1 %copy-start.3 = (bf16[1,192,3072]{2,1,0:T(8,128)(2,1)S(1)}, bf16[1,192,3072]{2,1,0:T(8,128)(2,1)}, u32[]{:S(2)}) copy-start(bf16[1,192,3072]{2,1,0:T(8,128)(2,1)} %param.15) | copy-start | bytes 3538948
Sparse Core Ops, SparseCore 0:
  10.7 224.8 all-gather.1
  322.6 175.7 all-reduce.2
where the time goes:
time: 510 us; the launch traced here: 509 us
  waiting for transfers between devices  289 us (57%)
  blocking collectives  134 us (26%)
  local copies, waits for them, and re-layouts  27.8 us (5%)
  matrix products  23.4 us (5%)
  between operations  17.3 us (3%)
  other arithmetic  12.3 us (2%)
    psum x1, waiting for transfers between devices, per_device(): scene_full = lax.psum(scene_dense, 'frame')  175 us
    all_gather x1, blocking collectives, per_device(): blocks = lax.all_gather(adapter_couple, 'frame', axis=0, tiled=True)  76 us
    all_gather x1, waiting for transfers between devices, per_device(): lax.all_gather(output_weight, 'fsdp', axis=0, tiled=True)  58.8 us
    all_to_all x1, waiting for transfers between devices, per_device(): lax.all_to_all(chosen.astype(jnp.bfloat16), 'fsdp', split_axis=0, concat_...  54 us
    all_to_all x1, blocking collectives, per_device(): lax.all_to_all(grad_terms, 'fsdp', split_axis=3, concat_axis=0, tiled=True)  42.7 us
    unnamed x1, blocking collectives  15.7 us
    unnamed x18, local copies, waits for them, and re-layouts  13 us
  transfers between devices with their start and end apart: 3, of which 3 were waited for; matrix products, arithmetic and copies ran while one was open for 3% of the time, Pallas kernels for 0%

commit v1 on v0

--- a/solution.py
+++ b/solution.py
@@ -108,7 +108,7 @@
     scene_dense = jnp.einsum(
         "fs,fxrd->sxrd", column_pick.astype(jnp.float32), pieces, precision=lax.Precision.HIGHEST
     )
-    scene_full = lax.psum(scene_dense, "frame")
+    scene_full = jnp.sum(lax.all_gather(scene_dense, "frame"), axis=0)
     owned_rows = lax.dynamic_slice_in_dim(scene_full, lax.axis_index("frame"), 1, 0)
     return (owned_rows[:, 0], owned_rows[:, 1], frame_loss)
 

time: 510 us -> 1030 us (2.02)
  waiting for transfers between devices: 289 us -> 801 us
  other arithmetic: 12.3 us -> 24 us
    all_gather x0 -> x1, waiting for transfers between devices: none -> 688 us  [per_device(): scene_full = jnp.sum(lax.all_gather(scene_dense, 'frame'), axis=0)]
    psum x1 -> x0, waiting for transfers between devices: 175 us -> none  [per_device(): scene_full = lax.psum(scene_dense, 'frame')]
    reduce_sum x0 -> x1, other arithmetic: none -> 13.1 us  [per_device(): scene_full = jnp.sum(lax.all_gather(scene_dense, 'frame'), axis=0)]
  transfers between devices with their start and end apart: 3 -> 3, of which waited for: 3 -> 3; matrix products, arithmetic and copies ran while one was open for 3% -> 2% of each run, Pallas kernels for 0% -> 0%
where the time goes in v1:
time: 1030 us
  waiting for transfers between devices  801 us (78%)
  blocking collectives  134 us (13%)
  local copies, waits for them, and re-layouts  27.5 us (3%)
  other arithmetic  24 us (2%)
  matrix products  22.5 us (2%)
  between operations  17.3 us (2%)
    all_gather x1, waiting for transfers between devices, per_device(): scene_full = jnp.sum(lax.all_gather(scene_dense, 'frame'), axis=0)  688 us
    all_gather x1, blocking collectives, per_device(): blocks = lax.all_gather(adapter_couple, 'frame', axis=0, tiled=True)  76 us
    all_gather x1, waiting for transfers between devices, per_device(): lax.all_gather(output_weight, 'fsdp', axis=0, tiled=True)  58.8 us
    all_to_all x1, waiting for transfers between devices, per_device(): lax.all_to_all(chosen.astype(jnp.bfloat16), 'fsdp', split_axis=0, concat_...  54 us
    all_to_all x1, blocking collectives, per_device(): lax.all_to_all(grad_terms, 'fsdp', split_axis=3, concat_axis=0, tiled=True)  42.7 us
  transfers between devices with their start and end apart: 3, of which 3 were waited for; matrix products, arithmetic and copies ran while one was open for 2% of the time, Pallas kernels for 0%

profile of v1, /device:TPU:16, one launch (start us, length us, event | category | flops | bytes accessed | tf_op | source)
XLA Modules:
  0.0 1031.9 jit_solution(17106012003785096691)
XLA Ops:
  8.6 1.3 dynamic-slice
  9.8 0.8 dynamic-update-slice
  10.6 15.7 %all-reduce = s32[16]{0:T(128)S(1)} all-reduce(s32[16]{0:T(128)S(1)} %dynamic-update-slice), channel_id=1, replica_groups=mesh['frame'=16,'fsdp'=16] {'fsdp'}, use_global_device_ids=true, to_apply=%add | all-reduce | flops 16 | bytes 128
  26.3 0.8 select_reduce_fusion
  27.1 0.8 pad_maximum_fusion.1
  27.9 76.0 %all_gather.17 = bf16[16,2,64,192]{3,2,1,0:T(8,128)(2,1)S(1)} all-gather(bf16[1,2,64,192]{3,2,1,0:T(8,128)(2,1)S(1)} %pad_maximum_fusion.1), channel_id=1, replica_groups=mesh['frame'=16,'fsdp'=16] {'frame'}, dimensions={0}, use_global_device_ids=true | all-gather | bytes 835584 | tf_op jit(solution)/shard_map/all_gather | solution.py:64
  103.9 0.7 convolution_convert_fusion
  104.6 1.3 copy.59
  106.0 4.8 all-to-all-start
  111.7 1.6 copy.71
  113.6 0.8 fusion.24
  114.4 2.0 fusion.51
  116.3 1.1 fusion.15
  117.5 1.8 copy.56
  119.3 54.0 %all-to-all-done = bf16[16,2,64,192]{3,2,1,0:T(8,128)(2,1)S(1)} async-done(((bf16[16,2,64,192]{3,2,1,0:T(8,128)(2,1)}), bf16[16,2,64,192]{3,2,1,0:T(8,128)(2,1)S(1)}, u32[]{:S(2)}, u32[]{:S(2)}) %all-to-all-start) | async-done | bytes 786464 | tf_op jit(solution)/shard_map/all_to_all | solution.py:71
  173.9 1.1 all_to_all.29
  175.0 1.8 fusion.33
  176.8 58.8 %all-gather.4.cloned.1.call-done = bf16[3072,3072]{1,0:T(8,128)(2,1)} async-done(((bf16[192,3072]{1,0:T(8,128)(2,1)}), bf16[3072,3072]{1,0:T(8,128)(2,1)}) %all-gather.4.cloned.1.call-update) | async-done | bytes 18874384 | tf_op jit(solution)/shard_map/all_gather | solution.py:55
  235.6 9.1 fusion.5
  244.7 1.5 multiply_reduce_fusion
  246.2 3.2 convolution_bitcast_fusion.1
  249.7 0.7 copy-done.4
  250.5 1.3 pad_maximum_fusion
  251.7 4.4 copy.61
  256.2 4.2 reshape.121
  260.4 42.7 %all_to_all.36 = f32[16,1,24576]{2,1,0:T(1,128)S(1)} all-to-all(f32[16,1,24576]{2,1,0:T(1,128)} %reshape.121), channel_id=1, replica_groups=mesh['frame'=16,'fsdp'=16] {'fsdp'}, dimensions={0} | all-to-all | bytes 3145728 | tf_op jit(solution)/shard_map/all_to_all | solution.py:107
  303.7 6.0 reduce.5
  309.7 3.4 reshape.122
  313.1 3.8 copy.69
  316.9 4.0 fusion.12
  321.6 687.9 %all-gather.6.cloned.1.call-done = f32[256,2,64,192]{3,0,2,1:T(8,128)} async-done(((f32[16,2,64,192]{3,0,2,1:T(8,128)}), f32[256,2,64,192]{3,0,2,1:T(8,128)}) %all-gather.6.cloned.1.call-update) | async-done | bytes 25165840 | tf_op jit(solution)/shard_map/all_gather | solution.py:111
  1009.5 13.1 %reduce_sum.40 = f32[16,2,64,192]{3,0,2,1:T(8,128)S(1)} reduce(f32[16,16,2,64,192]{4,1,0,3,2:T(8,128)} %bitcast.98, f32[]{:T(128)} %constant.3.clone.1), dimensions={0}, to_apply=%region_3.4 | reduce | flops 5898240 | bytes 26738692 | tf_op jit(solution)/shard_map/reduce_sum | solution.py:111
  (23 shorter events, 4.1 us)
Async XLA Ops:
  7.2 228.4 %all-gather.4.cloned.1.call-start = ((), (), s32[]{:S(2)}) async-start(), calls=%async_computation.2 | async-start | bytes 20054016 | tf_op jit(solution)/shard_map/all_gather | solution.py:55
  104.6 6.9 copy-start
  106.0 67.3 %all-to-all-start = ((bf16[16,2,64,192]{3,2,1,0:T(8,128)(2,1)}), bf16[16,2,64,192]{3,2,1,0:T(8,128)(2,1)S(1)}, u32[]{:S(2)}, u32[]{:S(2)}) async-start(bf16[16,2,64,192]{3,2,1,0:T(8,128)(2,1)} %copy.59), calls=%async_computation | async-start | bytes 2097152 | tf_op jit(solution)/shard_map/all_to_all | solution.py:71
  110.8 898.7 %all-gather.6.cloned.1.call-start = ((), (), s32[]{:S(2)}) async-start(), calls=%async_computation.3 | async-start | bytes 35651584 | tf_op jit(solution)/shard_map/all_gather | solution.py:111
  111.5 1.8 copy-start.1
  173.9 61.7 %copy-start.2 = (bf16[1,192,24,128]{3,2,1,0:T(8,128)(2,1)S(1)}, bf16[1,192,24,128]{3,2,1,0:T(8,128)(2,1)}, u32[]{:S(2)}) copy-start(bf16[1,192,24,128]{3,2,1,0:T(8,128)(2,1)} %copy.56) | copy-start | bytes 3538948
  235.6 9.1 copy-start.3
  249.4 1.1 copy-start.4
Sparse Core Ops, SparseCore 0:
  10.7 224.8 all-gather.3
  321.1 688.3 all-gather.5
